TPU v7x, 256 devices: a whole 4x4x8 slice. The times are simulated.
256 devices in a mesh: gx: 16 (over x_lo, y, core), yz: 16 (over z, x_hi).
Axes of the slice: x: 4 (x_hi: 2, x_lo: 2; x = x_hi * 2 + x_lo), y: 4, z: 8, core: 2. Of those that a mesh axis runs over, the one named last changes fastest.
Arguments:
- volume: bfloat16 [128, 16, 128, 128], P('gx', None, 'yz'), may hold values from -6 to 6
- weight_one: bfloat16 [32, 432], replicated, may hold values from -0.875 to 0.875
- weight_two: bfloat16 [64, 864], replicated, may hold values from -0.625 to 0.625
- weight_three: bfloat16 [128, 1728], replicated, may hold values from -0.21875 to 0.21875
Outputs:
- features: bfloat16 [128, 32, 1024], P('yz', 'gx')
All inputs are finite; a program needn't handle non-finite values.
Results may differ from a plain program's by a relative error of at most 0.0053.
Values may be sent and summed in bfloat16 or wider, within the bound.
A program may use at most 64 MiB of HBM per device.

v0:
```python
import jax
import jax.numpy as jnp
from jax import lax
from jax.sharding import PartitionSpec as P


def with_halo(block, sides, width):
    for axis, dim in sides:
        count = lax.axis_size(axis)
        forward = [(i, i + 1) for i in range(count - 1)]
        backward = [(target, source) for source, target in forward]
        low = lax.ppermute(
            lax.slice_in_dim(block, block.shape[dim] - width, None, axis=dim), axis, forward
        )
        high = lax.ppermute(lax.slice_in_dim(block, 0, width, axis=dim), axis, backward)
        block = jnp.concatenate([low, block, high], axis=dim)
    return block


def block_conv(padded, weight):
    in_rows = weight.shape[1] // 27
    kernel = weight.reshape(weight.shape[0], 3, 3, 3, in_rows)
    result = lax.conv_general_dilated(
        padded[None],
        kernel,
        (1, 1, 1),
        "VALID",
        dimension_numbers=("NDCHW", "ODHWI", "NDCHW"),
        preferred_element_type=jnp.float32,
    )
    return result[0]


def conv_pool(padded, weight):
    activated = jax.nn.relu(block_conv(padded, weight))
    planes, rows, height, breadth = activated.shape
    grouped = activated.reshape(planes // 2, 2, rows, height // 2, 2, breadth // 2, 2)
    return (jnp.sum(grouped, axis=(1, 4, 6)) * 0.125).astype(jnp.bfloat16)


def conv_planes(padded, weight):
    result = block_conv(padded, weight)
    planes, rows, height, breadth = result.shape
    return result.reshape(planes, rows, height * breadth)


def face_cells(block):
    grown = with_halo(block, (("gx", 0), ("yz", 2)), 1)
    return jnp.pad(grown, ((0, 0), (0, 0), (0, 0), (1, 1)))


def per_device(volume, weight_one, weight_two, weight_three):
    pooled_one = conv_pool(face_cells(volume), weight_one)
    pooled_two = conv_pool(face_cells(pooled_one), weight_two)
    shards = lax.axis_size("yz")
    out_rows = weight_three.shape[0] // shards
    grown = with_halo(pooled_two, (("gx", 0),), 1)
    whole = lax.all_gather(grown, "yz", axis=2, tiled=True)
    whole = jnp.pad(whole, ((0, 0), (0, 0), (1, 1), (1, 1)))
    picked = lax.dynamic_slice_in_dim(weight_three, lax.axis_index("yz") * out_rows, out_rows, 0)
    summed = jnp.moveaxis(conv_planes(whole, picked), 0, 1)
    return jax.nn.relu(summed).astype(jnp.bfloat16)


def solution(mesh):
    placed = (P("gx", None, "yz", None), P(), P(), P())
    return jax.shard_map(
        per_device, mesh=mesh, in_specs=placed, out_specs=P("yz", "gx", None), check_vma=False
    )
```

profile of v0, /device:TPU:2, one launch (start us, length us, event | category | flops | bytes accessed | tf_op | source)
XLA Modules:
  0.0 144.3 jit_solution(10215442351459870463)
XLA Ops:
  0.0 0.8 fusion.64
  0.8 1.9 %collective-permute-start = (bf16[1,16,8,128]{3,2,1,0:T(8,128)(2,1)S(1)}, bf16[1,16,8,128]{3,2,1,0:T(8,128)(2,1)S(1)}, u32[]{:S(2)}, u32[]{:S(2)}) collective-permute-start(bf16[1,16,8,128]{3,2,1,0:T(8,128)(2,1)S(1)} %get-tuple-element.12), channel_id=1, source_target_pairs={{0,16},{16,32},{32,48},{48,64},{64,80},{80,96},{96,112},{112,128},... | collective-permute-start | bytes 98312 | tf_op jit(solution)/shard_map/ppermute | solution.py:12
  2.8 5.8 %collective-permute-start.1 = (bf16[1,16,8,128]{3,2,1,0:T(8,128)(2,1)S(1)}, bf16[1,16,8,128]{3,2,1,0:T(8,128)(2,1)S(1)}, u32[]{:S(2)}, u32[]{:S(2)}) collective-permute-start(bf16[1,16,8,128]{3,2,1,0:T(8,128)(2,1)S(1)} %get-tuple-element.11), channel_id=1, source_target_pairs={{16,0},{32,16},{48,32},{64,48},{80,64},{96,80},{112,96},{128,112},... | collective-permute-start | bytes 98312 | tf_op jit(solution)/shard_map/ppermute | solution.py:15
  8.5 1.0 constant_dynamic-update-slice_fusion.1
  9.5 0.6 collective-permute-done.1
  10.2 4.0 %collective-permute-start.2 = (bf16[10,16,1,128]{3,2,1,0:T(2,128)(2,1)S(1)}, bf16[10,16,1,128]{3,2,1,0:T(2,128)(2,1)S(1)}, u32[]{:S(2)}, u32[]{:S(2)}) collective-permute-start(bf16[10,16,1,128]{3,2,1,0:T(2,128)(2,1)S(1)} %get-tuple-element.7), channel_id=1, source_target_pairs={{0,1},{1,2},{2,3},{3,4},{4,5},{5,6},{6,7},{7,8},{8,9},{9,10},{10,1... | collective-permute-start | bytes 122888 | tf_op jit(solution)/shard_map/ppermute | solution.py:12
  14.3 1.3 collective-permute-start.3
  15.6 0.9 copy.59
  16.5 5.6 %collective-permute-done.3 = bf16[10,16,1,128]{3,2,1,0:T(2,128)(2,1)S(1)} collective-permute-done((bf16[10,16,1,128]{3,2,1,0:T(2,128)(2,1)S(1)}, bf16[10,16,1,128]{3,2,1,0:T(2,128)(2,1)S(1)}, u32[]{:S(2)}, u32[]{:S(2)}) %collective-permute-start.3) | collective-permute-done | bytes 40992 | tf_op jit(solution)/shard_map/ppermute | solution.py:15
  22.1 1.2 fusion.35
  23.6 3.7 %reshape.59 = bf16[10,16,10,1,8,17]{5,4,2,1,0,3:T(8,128)(2,1)} reshape(bf16[10,16,10,1,136]{4,2,1,0,3:T(8,128)(2,1)S(1)} %pad.15) | data formatting | bytes 870400 | tf_op jit(solution)/shard_map/conv_general_dilated | solution.py:23
  27.3 7.9 %copy.58 = bf16[10,16,10,1,8,17]{1,4,5,2,0,3:T(8,128)(2,1)} copy(bf16[10,16,10,1,8,17]{5,4,2,1,0,3:T(8,128)(2,1)} %reshape.59) | data formatting | bytes 870400 | tf_op jit(solution)/shard_map/conv_general_dilated | solution.py:23
  35.2 1.1 slice.48
  36.4 7.3 %select_maximum_fusion = f32[8,8,8,17,32]{4,2,3,1,0:T(8,128)S(1)} fusion(pred[8,17]{0,1:T(8,128)(4,1)S(1)} %copy-done.2, bf16[32,3,3,3,16]{0,4,3,2,1:T(8,128)(2,1)S(1)} %bitcast.57, bf16[10,16,10,1,7,2]{1,4,5,2,0,3:T(8,128)(2,1)S(1)} %slice.48, bf16[10,16,10,1,8,17]{1,4,5,2,0,3:T(8,128)(2,1)} %copy.58), kind=kOutput, calls=%fused_computation.2 | convolution fusion | flops 242664448 | bytes 1621896 | tf_op jit(solution)/shard_map/conv_general_dilated | solution.py:23
  43.7 0.8 copy.60
  44.5 2.2 %slice.49 = f32[8,8,1,128,32]{4,1,3,0,2:T(8,128)} slice(f32[8,8,1,136,32]{4,1,3,0,2:T(8,128)S(1)} %bitcast.47), slice={[0:8], [0:8], [0:1], [0:128], [0:32]} | slice | bytes 2097152 | tf_op jit(solution)/shard_map/jit(relu)/max | solution.py:35
  46.7 5.0 %reduce_sum.18 = f32[4,32,4,64]{1,2,3,0:T(4,128)S(1)} reduce(f32[4,2,32,4,2,64,2]{2,4,3,6,5,1,0:T(2,128)} %bitcast.48, f32[]{:T(128)} %constant.8.clone.1), dimensions={1,4,6}, to_apply=%region_0.1 | reduce | flops 229376 | bytes 1179652 | tf_op jit(solution)/shard_map/reduce_sum | solution.py:38
  51.9 1.9 %collective-permute-start.4 = (bf16[1,32,4,64]{1,2,3,0:T(4,128)(2,1)S(1)}, bf16[1,32,4,64]{1,2,3,0:T(4,128)(2,1)S(1)}, u32[]{:S(2)}, u32[]{:S(2)}) collective-permute-start(bf16[1,32,4,64]{1,2,3,0:T(4,128)(2,1)S(1)} %get-tuple-element.9), channel_id=1, source_target_pairs={{0,16},{16,32},{32,48},{48,64},{64,80},{80,96},{96,112},{112,128},... | collective-permute-start | bytes 49160 | tf_op jit(solution)/shard_map/ppermute | solution.py:12
  53.8 5.8 %collective-permute-start.5 = (bf16[1,32,4,64]{1,2,3,0:T(4,128)(2,1)S(1)}, bf16[1,32,4,64]{1,2,3,0:T(4,128)(2,1)S(1)}, u32[]{:S(2)}, u32[]{:S(2)}) collective-permute-start(bf16[1,32,4,64]{1,2,3,0:T(4,128)(2,1)S(1)} %get-tuple-element.10), channel_id=1, source_target_pairs={{16,0},{32,16},{48,32},{64,48},{80,64},{96,80},{112,96},{128,112},... | collective-permute-start | bytes 49160 | tf_op jit(solution)/shard_map/ppermute | solution.py:15
  59.6 1.9 %collective-permute-done.5 = bf16[1,32,4,64]{1,2,3,0:T(4,128)(2,1)S(1)} collective-permute-done((bf16[1,32,4,64]{1,2,3,0:T(4,128)(2,1)S(1)}, bf16[1,32,4,64]{1,2,3,0:T(4,128)(2,1)S(1)}, u32[]{:S(2)}, u32[]{:S(2)}) %collective-permute-start.5) | collective-permute-done | bytes 16416 | tf_op jit(solution)/shard_map/ppermute | solution.py:15
  62.1 5.8 %collective-permute-start.6 = (bf16[6,32,1,64]{1,2,3,0:T(2,128)(2,1)S(1)}, bf16[6,32,1,64]{1,2,3,0:T(2,128)(2,1)S(1)}, u32[]{:S(2)}, u32[]{:S(2)}) collective-permute-start(bf16[6,32,1,64]{1,2,3,0:T(2,128)(2,1)S(1)} %get-tuple-element.5), channel_id=1, source_target_pairs={{0,1},{1,2},{2,3},{3,4},{4,5},{5,6},{6,7},{7,8},{8,9},{9,10},{10,1... | collective-permute-start | bytes 73736 | tf_op jit(solution)/shard_map/ppermute | solution.py:12
  67.9 1.3 collective-permute-start.7
  69.6 3.6 %collective-permute-done.6 = bf16[6,32,1,64]{1,2,3,0:T(2,128)(2,1)S(1)} collective-permute-done((bf16[6,32,1,64]{1,2,3,0:T(2,128)(2,1)S(1)}, bf16[6,32,1,64]{1,2,3,0:T(2,128)(2,1)S(1)}, u32[]{:S(2)}, u32[]{:S(2)}) %collective-permute-start.6) | collective-permute-done | bytes 24608 | tf_op jit(solution)/shard_map/ppermute | solution.py:12
  73.3 3.6 %collective-permute-done.7 = bf16[6,32,1,64]{1,2,3,0:T(2,128)(2,1)S(1)} collective-permute-done((bf16[6,32,1,64]{1,2,3,0:T(2,128)(2,1)S(1)}, bf16[6,32,1,64]{1,2,3,0:T(2,128)(2,1)S(1)}, u32[]{:S(2)}, u32[]{:S(2)}) %collective-permute-start.7) | collective-permute-done | bytes 24608 | tf_op jit(solution)/shard_map/ppermute | solution.py:15
  78.2 1.4 fusion.36
  80.3 1.9 %collective-permute-start.8 = (bf16[1,64,2,32]{1,2,3,0:T(2,128)(2,1)S(1)}, bf16[1,64,2,32]{1,2,3,0:T(2,128)(2,1)S(1)}, u32[]{:S(2)}, u32[]{:S(2)}) collective-permute-start(bf16[1,64,2,32]{1,2,3,0:T(2,128)(2,1)S(1)} %get-tuple-element.13), channel_id=1, source_target_pairs={{0,16},{16,32},{32,48},{48,64},{64,80},{80,96},{96,112},{112,128},... | collective-permute-start | bytes 24584 | tf_op jit(solution)/shard_map/ppermute | solution.py:12
  82.2 5.8 %collective-permute-start.9 = (bf16[1,64,2,32]{1,2,3,0:T(2,128)(2,1)S(1)}, bf16[1,64,2,32]{1,2,3,0:T(2,128)(2,1)S(1)}, u32[]{:S(2)}, u32[]{:S(2)}) collective-permute-start(bf16[1,64,2,32]{1,2,3,0:T(2,128)(2,1)S(1)} %get-tuple-element.14), channel_id=1, source_target_pairs={{16,0},{32,16},{48,32},{64,48},{80,64},{96,80},{112,96},{128,112},... | collective-permute-start | bytes 24584 | tf_op jit(solution)/shard_map/ppermute | solution.py:15
  88.2 1.2 collective-permute-done.9
  89.5 48.7 %all_gather.3 = bf16[4,64,32,32]{1,3,0,2:T(8,128)(2,1)S(1)} all-gather(bf16[4,64,2,32]{1,3,0,2:T(8,128)(2,1)S(1)} %copy.69), channel_id=1, replica_groups=mesh['gx'=16,'yz'=16] {'yz'}, dimensions={2}, use_global_device_ids=true | all-gather | bytes 557056 | tf_op jit(solution)/shard_map/all_gather | solution.py:58
  139.2 0.7 pad.19.clone
  140.2 2.7 %fusion.30 = bf16[2,32,8,5,8]{4,2,3,1,0:T(8,128)(2,1)S(1)} fusion(bf16[8,3,3,3,64]{0,4,3,2,1:T(8,128)(2,1)S(1)} %bitcast.54, bf16[4,64,34,1,7,2]{1,4,5,2,0,3:T(8,128)(2,1)S(1)} %slice.58, bf16[4,64,34,1,8,5]{1,4,5,2,0,3:T(8,128)(2,1)S(1)} %copy.72, pred[8,5]{0,1:T(8,128)(4,1)S(1)} %copy-done.4), kind=kOutput, calls=%fused_computation.29 | convolution fusion | flops 73764864 | bytes 1008680 | tf_op jit(solution)/shard_map/conv_general_dilated | solution.py:23
  143.6 0.7 copy.77
  (47 shorter events, 6.0 us)
Async XLA Ops:
  0.0 88.0 %copy-start = (bf16[128,1728]{0,1:T(8,128)(2,1)S(1)}, bf16[128,1728]{0,1:T(8,128)(2,1)}, u32[]{:S(2)}) copy-start(bf16[128,1728]{0,1:T(8,128)(2,1)} %param.7) | copy-start | bytes 1327108
  0.8 7.7 %collective-permute-start = (bf16[1,16,8,128]{3,2,1,0:T(8,128)(2,1)S(1)}, bf16[1,16,8,128]{3,2,1,0:T(8,128)(2,1)S(1)}, u32[]{:S(2)}, u32[]{:S(2)}) collective-permute-start(bf16[1,16,8,128]{3,2,1,0:T(8,128)(2,1)S(1)} %get-tuple-element.12), channel_id=1, source_target_pairs={{0,16},{16,32},{32,48},{48,64},{64,80},{80,96},{96,112},{112,128},... | collective-permute-start | bytes 98312 | tf_op jit(solution)/shard_map/ppermute | solution.py:12
  2.8 7.3 %collective-permute-start.1 = (bf16[1,16,8,128]{3,2,1,0:T(8,128)(2,1)S(1)}, bf16[1,16,8,128]{3,2,1,0:T(8,128)(2,1)S(1)}, u32[]{:S(2)}, u32[]{:S(2)}) collective-permute-start(bf16[1,16,8,128]{3,2,1,0:T(8,128)(2,1)S(1)} %get-tuple-element.11), channel_id=1, source_target_pairs={{16,0},{32,16},{48,32},{64,48},{80,64},{96,80},{112,96},{128,112},... | collective-permute-start | bytes 98312 | tf_op jit(solution)/shard_map/ppermute | solution.py:15
  10.2 6.2 %collective-permute-start.2 = (bf16[10,16,1,128]{3,2,1,0:T(2,128)(2,1)S(1)}, bf16[10,16,1,128]{3,2,1,0:T(2,128)(2,1)S(1)}, u32[]{:S(2)}, u32[]{:S(2)}) collective-permute-start(bf16[10,16,1,128]{3,2,1,0:T(2,128)(2,1)S(1)} %get-tuple-element.7), channel_id=1, source_target_pairs={{0,1},{1,2},{2,3},{3,4},{4,5},{5,6},{6,7},{7,8},{8,9},{9,10},{10,1... | collective-permute-start | bytes 122888 | tf_op jit(solution)/shard_map/ppermute | solution.py:12
  14.3 7.8 %collective-permute-start.3 = (bf16[10,16,1,128]{3,2,1,0:T(2,128)(2,1)S(1)}, bf16[10,16,1,128]{3,2,1,0:T(2,128)(2,1)S(1)}, u32[]{:S(2)}, u32[]{:S(2)}) collective-permute-start(bf16[10,16,1,128]{3,2,1,0:T(2,128)(2,1)S(1)} %get-tuple-element.8), channel_id=1, source_target_pairs={{1,0},{2,1},{3,2},{4,3},{5,4},{6,5},{7,6},{8,7},{9,8},{10,9},{11,1... | collective-permute-start | bytes 122888 | tf_op jit(solution)/shard_map/ppermute | solution.py:15
  27.3 9.0 %copy-start.2 = (pred[8,17]{0,1:T(8,128)(4,1)S(1)}, pred[8,17]{0,1:T(8,128)(4,1)}, u32[]{:S(2)}) copy-start(pred[8,17]{0,1:T(8,128)(4,1)} %constant.44) | copy-start | bytes 412
  46.7 22.5 %copy-start.1 = (bf16[64,864]{1,0:T(8,128)(2,1)S(1)}, bf16[64,864]{1,0:T(8,128)(2,1)}, u32[]{:S(2)}) copy-start(bf16[64,864]{1,0:T(8,128)(2,1)} %param.6) | copy-start | bytes 331780
  51.9 7.7 %collective-permute-start.4 = (bf16[1,32,4,64]{1,2,3,0:T(4,128)(2,1)S(1)}, bf16[1,32,4,64]{1,2,3,0:T(4,128)(2,1)S(1)}, u32[]{:S(2)}, u32[]{:S(2)}) collective-permute-start(bf16[1,32,4,64]{1,2,3,0:T(4,128)(2,1)S(1)} %get-tuple-element.9), channel_id=1, source_target_pairs={{0,16},{16,32},{32,48},{48,64},{64,80},{80,96},{96,112},{112,128},... | collective-permute-start | bytes 49160 | tf_op jit(solution)/shard_map/ppermute | solution.py:12
  53.8 7.6 %collective-permute-start.5 = (bf16[1,32,4,64]{1,2,3,0:T(4,128)(2,1)S(1)}, bf16[1,32,4,64]{1,2,3,0:T(4,128)(2,1)S(1)}, u32[]{:S(2)}, u32[]{:S(2)}) collective-permute-start(bf16[1,32,4,64]{1,2,3,0:T(4,128)(2,1)S(1)} %get-tuple-element.10), channel_id=1, source_target_pairs={{16,0},{32,16},{48,32},{64,48},{80,64},{96,80},{112,96},{128,112},... | collective-permute-start | bytes 49160 | tf_op jit(solution)/shard_map/ppermute | solution.py:15
  62.1 11.1 %collective-permute-start.6 = (bf16[6,32,1,64]{1,2,3,0:T(2,128)(2,1)S(1)}, bf16[6,32,1,64]{1,2,3,0:T(2,128)(2,1)S(1)}, u32[]{:S(2)}, u32[]{:S(2)}) collective-permute-start(bf16[6,32,1,64]{1,2,3,0:T(2,128)(2,1)S(1)} %get-tuple-element.5), channel_id=1, source_target_pairs={{0,1},{1,2},{2,3},{3,4},{4,5},{5,6},{6,7},{7,8},{8,9},{9,10},{10,1... | collective-permute-start | bytes 73736 | tf_op jit(solution)/shard_map/ppermute | solution.py:12
  67.9 9.1 %collective-permute-start.7 = (bf16[6,32,1,64]{1,2,3,0:T(2,128)(2,1)S(1)}, bf16[6,32,1,64]{1,2,3,0:T(2,128)(2,1)S(1)}, u32[]{:S(2)}, u32[]{:S(2)}) collective-permute-start(bf16[6,32,1,64]{1,2,3,0:T(2,128)(2,1)S(1)} %get-tuple-element.6), channel_id=1, source_target_pairs={{1,0},{2,1},{3,2},{4,3},{5,4},{6,5},{7,6},{8,7},{9,8},{10,9},{11,1... | collective-permute-start | bytes 73736 | tf_op jit(solution)/shard_map/ppermute | solution.py:15
  77.1 1.1 copy-start.3
  80.3 7.9 %collective-permute-start.8 = (bf16[1,64,2,32]{1,2,3,0:T(2,128)(2,1)S(1)}, bf16[1,64,2,32]{1,2,3,0:T(2,128)(2,1)S(1)}, u32[]{:S(2)}, u32[]{:S(2)}) collective-permute-start(bf16[1,64,2,32]{1,2,3,0:T(2,128)(2,1)S(1)} %get-tuple-element.13), channel_id=1, source_target_pairs={{0,16},{16,32},{32,48},{48,64},{64,80},{80,96},{96,112},{112,128},... | collective-permute-start | bytes 24584 | tf_op jit(solution)/shard_map/ppermute | solution.py:12
  82.2 7.2 %collective-permute-start.9 = (bf16[1,64,2,32]{1,2,3,0:T(2,128)(2,1)S(1)}, bf16[1,64,2,32]{1,2,3,0:T(2,128)(2,1)S(1)}, u32[]{:S(2)}, u32[]{:S(2)}) collective-permute-start(bf16[1,64,2,32]{1,2,3,0:T(2,128)(2,1)S(1)} %get-tuple-element.14), channel_id=1, source_target_pairs={{16,0},{32,16},{48,32},{64,48},{80,64},{96,80},{112,96},{128,112},... | collective-permute-start | bytes 24584 | tf_op jit(solution)/shard_map/ppermute | solution.py:15
  139.2 1.0 copy-start.4
where the time goes:
time: 145 us; the launch traced here: 144 us
  blocking collectives  48.7 us (34%)
  starting transfers between devices  35.4 us (24%)
  local copies, waits for them, and re-layouts  24.6 us (17%)
  waiting for transfers between devices  16.5 us (11%)
  matrix products  11.3 us (8%)
  other arithmetic  7.46 us (5%)
    all_gather x1, blocking collectives, per_device(): whole = lax.all_gather(grown, 'yz', axis=2, tiled=True)  48.7 us
    ppermute x5, starting transfers between devices, with_halo(): lax.ppermute(lax.slice_in_dim(block, 0, width, axis=dim), axis, backward)  19.8 us
    ppermute x5, starting transfers between devices, with_halo(): lax.ppermute(lax.slice_in_dim(block, block.shape[dim] - width, None, axis...  15.5 us
    conv_general_dilated x7, local copies, waits for them, and re-layouts, block_conv(): lax.conv_general_dilated(padded[None], kernel, (1, 1, 1), 'VALID', dimens...  13.2 us
    ppermute x5, waiting for transfers between devices, with_halo(): lax.ppermute(lax.slice_in_dim(block, 0, width, axis=dim), axis, backward)  12.9 us
    conv_general_dilated x3, matrix products, block_conv(): lax.conv_general_dilated(padded[None], kernel, (1, 1, 1), 'VALID', dimens...  11.3 us
    reduce_sum x2, other arithmetic, conv_pool(): return (jnp.sum(grouped, axis=(1, 4, 6)) * 0.125).astype(jnp.bfloat16)  5.47 us
    ppermute x5, waiting for transfers between devices, with_halo(): lax.ppermute(lax.slice_in_dim(block, block.shape[dim] - width, None, axis...  3.6 us
  transfers between devices with their start and end apart: 10, of which 6 were waited for; matrix products, arithmetic and copies ran while one was open for 2% of the time, Pallas kernels for 0%

commit v1 on v0

v1 whole, which is shorter than its diff:
```python
import functools

import jax
import jax.numpy as jnp
from jax import lax
from jax.experimental import pallas as pl
from jax.experimental.pallas import tpu as pltpu
from jax.sharding import PartitionSpec as P

MESH = pl.DeviceIdType.MESH
BF = jnp.bfloat16
F32 = jnp.float32
AROUND = tuple((dx, dy) for dx in (-1, 0, 1) for dy in (-1, 0, 1) if (dx, dy) != (0, 0))


def iota(shape, axis):
    return lax.broadcasted_iota(jnp.int32, shape, axis)


def choose(rows, target):
    return jnp.where(iota((rows, target.shape[1]), 0) == target, 1.0, 0.0).astype(BF)


def dot(a, b):
    return jnp.dot(a, b, preferred_element_type=F32)


def shifted(block, lane, low, high):
    zero = jnp.zeros_like(block)
    up = jnp.where(lane == low, zero, pltpu.roll(block, 1, 1))
    down = jnp.where(lane == high, zero, pltpu.roll(block, 127, 1))
    return up, down


def spread_one(w1, w1t):
    column = iota((1, 480), 1)
    c = (column >= 160).astype(jnp.int32) + (column >= 320).astype(jnp.int32)
    pos = column - 160 * c
    own = pos < 128
    y = jnp.where(own, pos & 7, jnp.where(pos < 144, -1, 8))
    i = jnp.where(own, pos >> 3, pos & 15)
    for out in range(8):
        b = y - out + 1
        target = jnp.where((b >= 0) & (b <= 2), 32 + b * 48 + c * 16 + i, -1)
        chosen = choose(176, target)
        row = (out % 2) * 128 + (out // 2) * 32
        for a, (start, skip) in enumerate(((0, 32), (128, 16), (256, 0))):
            part = dot(w1[:, start:144 * a + 144], chosen[skip:, :])
            w1t[a, row:row + 32, :] = part.astype(BF)


def spread_two(w2, w2t):
    column = iota((1, 576), 1)
    c = (column >= 192).astype(jnp.int32) + (column >= 384).astype(jnp.int32)
    pos = column - 192 * c
    group = pos >> 5
    y = jnp.where(group < 4, group, jnp.where(group == 4, -1, 4))
    i = pos & 31
    for out in range(4):
        b = y - out + 1
        target = jnp.where((b >= 0) & (b <= 2), 64 + b * 96 + c * 32 + i, -1)
        chosen = choose(352, target)
        row = (out % 2) * 128 + (out // 2) * 64
        for a, (start, skip) in enumerate(((0, 64), (256, 32), (512, 0))):
            part = dot(w2[:, start:288 * a + 288], chosen[skip:, :])
            w2t[a, row:row + 64, :] = part.astype(BF)


def spread_three(shards, w3, w3t):
    column = iota((1, 384), 1)
    c = (column >= 128).astype(jnp.int32) + (column >= 256).astype(jnp.int32)
    pos = column - 128 * c
    y = pos >> 6
    i = pos & 63
    size = 128 // shards
    for t, outs in enumerate(((0, 2), (1, -1))):
        parts = [[], [], []]
        for out in outs:
            b = y - out + 1
            target = jnp.where((b >= 0) & (b <= 2), b * 192 + c * 64 + i, -1)
            chosen = choose(576, target)
            for a in range(3):
                parts[a].append(lax.dot_general(
                    w3[a * 576:(a + 1) * 576, :], chosen, (((0,), (0,)), ((), ())),
                    preferred_element_type=F32))
        for a in range(3):
            both = jnp.stack([p.reshape(shards, size, 384) for p in parts[a]], axis=1)
            w3t[t, :, a * 384:(a + 1) * 384] = both.reshape(256, 384).astype(BF)


def kernel(groups, shards, v_hbm, w1_hbm, w2_hbm, w3_hbm, o_ref,
           p, w1, w2, w3, face, b1, w1t, q, b2e, b2o, w2t, w3t, out_s, in_s,
           load_sem, s1, r1, s2, r2, s3, r3):
    g = lax.axis_index("gx")
    s = lax.axis_index("yz")
    size = 128 // shards

    def at(dx, dy):
        return {"gx": lax.rem(g + dx + groups, groups), "yz": lax.rem(s + dy + shards, shards)}

    barrier = pltpu.get_barrier_semaphore()
    partners = [(dx, dy) for dx, dy in AROUND if dx != 0] + [(0, k) for k in range(1, shards)]
    for dx, dy in partners:
        pl.semaphore_signal(barrier, inc=1, device_id=at(dx, dy), device_id_type=MESH)

    loads = [
        pltpu.make_async_copy(v_hbm, p.at[1:9, 0:128], load_sem.at[0]),
        pltpu.make_async_copy(w1_hbm, w1, load_sem.at[1]),
        pltpu.make_async_copy(w2_hbm, w2, load_sem.at[2]),
        pltpu.make_async_copy(w3_hbm, w3, load_sem.at[3]),
    ]
    for load in loads:
        load.start()

    loads[0].wait()
    which = iota((32, 128), 0)
    ends = jnp.where(iota((32, 128), 1) == (which & 15) * 8 + (which >> 4) * 7, 1.0, 0.0).astype(BF)
    for x in range(0, 8, 2):
        cells = dot(ends, jnp.concatenate([p[1 + x, 0:128, :], p[2 + x, 0:128, :]], axis=1)).astype(BF)
        for k in range(2):
            face[0, x + k] = cells[0:16, k * 128:(k + 1) * 128]
            face[1, x + k] = cells[16:32, k * 128:(k + 1) * 128]

    pl.semaphore_wait(barrier, len(partners))

    first = []
    for k, (dx, dy) in enumerate(AROUND):
        plane = 7 if dx > 0 else 0
        to = 0 if dx > 0 else 9
        side = 1 if dy > 0 else 0
        rows = slice(128, 144) if dy > 0 else slice(144, 160)
        if dy == 0:
            src, dst = p.at[1 + plane, 0:128], p.at[to, 0:128]
        elif dx == 0:
            src, dst = face.at[side], p.at[1:9, rows]
        else:
            src, dst = face.at[side, plane], p.at[to, rows]
        first.append(pltpu.make_async_remote_copy(
            src_ref=src, dst_ref=dst, send_sem=s1.at[k], recv_sem=r1.at[k],
            device_id=at(dx, dy), device_id_type=MESH))
    for copy in first:
        copy.start()

    loads[1].wait()
    spread_one(w1, w1t)
    loads[2].wait()
    spread_two(w2, w2t)

    for copy in first:
        copy.wait_recv()

    @pl.when(g == 0)
    def _():
        p[0] = jnp.zeros((160, 128), BF)

    @pl.when(g == groups - 1)
    def _():
        p[9] = jnp.zeros((160, 128), BF)

    @pl.when(s == 0)
    def _():
        p[:, 128:144, :] = jnp.zeros((10, 16, 128), BF)

    @pl.when(s == shards - 1)
    def _():
        p[:, 144:160, :] = jnp.zeros((10, 16, 128), BF)

    lane = iota((160, 128), 1)
    for x in range(10):
        mid = p[x]
        up, down = shifted(mid, lane, 0, 127)
        b1[x, 0:160] = up
        b1[x, 160:320] = mid
        b1[x, 320:480] = down
    pooled = []
    for x in range(0, 8, 2):
        total = None
        for a in range(3):
            part = dot(w1t[a], jnp.concatenate([b1[x + a], b1[x + a + 1]], axis=1))
            total = part if total is None else total + part
        total = jnp.maximum(total, 0.0)
        total = total[0:128] + total[128:256]
        total = total[:, 0:128] + total[:, 128:256]
        total = (total + pltpu.roll(total, 127, 1)) * 0.125
        pooled.append(total.astype(BF))
    lanes = iota((256, 128), 1)
    pick = jnp.where(iota((256, 128), 0) == (lanes >> 6) * 128 + (lanes & 63) * 2, 1.0, 0.0).astype(BF)
    for j in range(2):
        q[2 + j, 0:128, :] = dot(jnp.concatenate(pooled[2 * j:2 * j + 2], axis=1), pick).astype(BF)

    second = []
    for k, (dx, dy) in enumerate(AROUND):
        to = slice(2, 4) if dx == 0 else (slice(0, 2) if dx > 0 else slice(4, 6))
        if dy == 0:
            rows, into = slice(0, 128), slice(0, 128)
        elif dy > 0:
            rows, into = slice(96, 128), slice(128, 160)
        else:
            rows, into = slice(0, 32), slice(160, 192)
        second.append(pltpu.make_async_remote_copy(
            src_ref=q.at[2:4, rows], dst_ref=q.at[to, into], send_sem=s2.at[k], recv_sem=r2.at[k],
            device_id=at(dx, dy), device_id_type=MESH))
    for copy in second:
        copy.start()

    loads[3].wait()
    spread_three(shards, w3, w3t)

    for copy in second:
        copy.wait_recv()

    @pl.when(g == 0)
    def _():
        q[0:2] = jnp.zeros((2, 192, 128), BF)

    @pl.when(g == groups - 1)
    def _():
        q[4:6] = jnp.zeros((2, 192, 128), BF)

    @pl.when(s == 0)
    def _():
        q[:, 128:160, :] = jnp.zeros((6, 32, 128), BF)

    @pl.when(s == shards - 1)
    def _():
        q[:, 160:192, :] = jnp.zeros((6, 32, 128), BF)

    lane = iota((192, 128), 1) & 63
    half = iota((192, 128), 1) < 64
    for j in range(5):
        if j > 0:
            mid = q[j]
            up, down = shifted(mid, lane, 0, 63)
            b2e[j - 1, 0:192] = up
            b2e[j - 1, 192:384] = mid
            b2e[j - 1, 384:576] = down
        mid = jnp.where(half, pltpu.roll(q[j], 64, 1), pltpu.roll(q[j + 1], 64, 1))
        up, down = shifted(mid, lane, 0, 63)
        b2o[j, 0:192] = up
        b2o[j, 192:384] = mid
        b2o[j, 384:576] = down
    pooled = []
    for j in range(0, 4, 2):
        total = dot(w2t[0], jnp.concatenate([b2o[j], b2o[j + 1]], axis=1))
        total += dot(w2t[1], jnp.concatenate([b2e[j], b2e[j + 1]], axis=1))
        total += dot(w2t[2], jnp.concatenate([b2o[j + 1], b2o[j + 2]], axis=1))
        total = jnp.maximum(total, 0.0)
        total = total[0:128] + total[128:256]
        for k in range(2):
            pair = total[:, k * 128:(k + 1) * 128]
            pair = pair + pltpu.roll(pair, 64, 1)
            pair = (pair + pltpu.roll(pair, 127, 1)) * 0.125
            if j + k == 0:
                pair = jnp.where(g == 0, 0.0, pair)
            if j + k == 3:
                pair = jnp.where(g == groups - 1, 0.0, pair)
            pooled.append(pair)

    low = iota((128, 128), 1) < 64
    stacked = jnp.concatenate(
        [jnp.where(low, pooled[a], pooled[a + 1]).astype(BF) for a in range(3)], axis=0)
    column = iota((1, 384), 1)
    c = column >> 7
    inside = column & 127
    z = (inside & 31) + c - 1
    target = jnp.where((z >= 0) & (z < 32), (inside >> 6) * 64 + 2 * z, -1)
    planes = dot(stacked, choose(128, target)).astype(BF)
    right = jnp.concatenate(
        [planes[a * 128:(a + 1) * 128, c * 128:(c + 1) * 128] for a in range(3) for c in range(3)], axis=0)
    even = dot(w3t[0], right)
    odd = dot(w3t[1], right)
    parity = (iota((256, 128), 1) & 32) == 0
    out_s[...] = jnp.where(parity, even, odd).astype(BF).reshape(shards, 2 * size, 128)

    third = []
    for k in range(1, shards):
        there = at(0, k)
        third.append(pltpu.make_async_remote_copy(
            src_ref=out_s.at[there["yz"]], dst_ref=in_s.at[s], send_sem=s3.at[k], recv_sem=r3.at[k],
            device_id=there, device_id_type=MESH))
    for copy in third:
        copy.start()
    in_s[s] = out_s[s]
    for copy in first + second:
        copy.wait_send()
    for copy in third:
        copy.wait_recv()

    low = iota((size, 128), 1) < 64
    parity = (iota((size, 128), 1) & 32) == 0
    done = []
    for n in range(shards):
        below = in_s[n - 1, size:, :].astype(F32) if n > 0 else jnp.zeros((size, 128), F32)
        above = in_s[n + 1, size:, :].astype(F32) if n < shards - 1 else jnp.zeros((size, 128), F32)
        whole = in_s[n, 0:size, :].astype(F32) + jnp.where(parity, below, above)
        done.append(jnp.maximum(whole, 0.0))
    for n in range(0, shards, 2):
        at0 = jnp.where(low, done[n], pltpu.roll(done[n + 1], 64, 1))
        at1 = jnp.where(low, pltpu.roll(done[n], 64, 1), done[n + 1])
        o_ref[0, :, n * 64:n * 64 + 128] = at0.astype(BF)
        o_ref[1, :, n * 64:n * 64 + 128] = at1.astype(BF)
    for copy in third:
        copy.wait_send()


def per_device(volume, weight_one, weight_two, weight_three):
    groups, shards = lax.axis_size("gx"), lax.axis_size("yz")
    size = 128 // shards
    anywhere = pl.BlockSpec(memory_space=pl.ANY)
    dma = pltpu.SemaphoreType.DMA
    out = pl.pallas_call(
        functools.partial(kernel, groups, shards),
        out_shape=jax.ShapeDtypeStruct((2, size, shards * 64), BF),
        in_specs=[anywhere] * 4,
        out_specs=pl.BlockSpec(memory_space=pltpu.VMEM),
        scratch_shapes=[
            pltpu.VMEM((10, 160, 128), BF),
            pltpu.VMEM((32, 432), BF),
            pltpu.VMEM((64, 864), BF),
            pltpu.VMEM((1728, 128), BF),
            pltpu.VMEM((2, 8, 16, 128), BF),
            pltpu.VMEM((10, 480, 128), BF),
            pltpu.VMEM((3, 256, 480), BF),
            pltpu.VMEM((6, 192, 128), BF),
            pltpu.VMEM((4, 576, 128), BF),
            pltpu.VMEM((5, 576, 128), BF),
            pltpu.VMEM((3, 256, 576), BF),
            pltpu.VMEM((2, 256, 1152), BF),
            pltpu.VMEM((shards, 2 * size, 128), BF),
            pltpu.VMEM((shards, 2 * size, 128), BF),
            dma((4,)),
            dma((8,)), dma((8,)), dma((8,)), dma((8,)),
            dma((shards,)), dma((shards,)),
        ],
        compiler_params=pltpu.CompilerParams(collective_id=0, has_side_effects=True),
    )(volume.reshape(8, 128, 128), weight_one, weight_two, weight_three.T)
    return jnp.moveaxis(out, 0, 1)


def solution(mesh):
    placed = (P("gx", None, "yz", None), P(), P(), P())
    return jax.shard_map(
        per_device, mesh=mesh, in_specs=placed, out_specs=P("yz", "gx", None), check_vma=False
    )
```

time: 145 us -> 31.8 us (0.22)
  the two profiles are of different devices: /device:TPU:2 before, /device:TPU:1 now
where the time goes in v1:
time: 31.8 us; the launch traced here: 31.6 us
  Pallas kernels  30.2 us (95%)
  local copies, waits for them, and re-layouts  1.41 us (4%)
    pallas_call x1, Pallas kernels, per_device(): pl.pallas_call(functools.partial(kernel, groups, shards), out_shape=jax.S...  30.2 us
    transpose x1, local copies, waits for them, and re-layouts, per_device(): return jnp.moveaxis(out, 0, 1)  1.41 us

profile of v1, /device:TPU:1, one launch (start us, length us, event | category | flops | bytes accessed | tf_op | source)
XLA Modules:
  0.0 31.6 jit_solution(5443005234891620407)
XLA Ops:
  0.0 30.2 %shard_map.46 = bf16[2,8,1024]{2,1,0:T(8,128)(2,1)} custom-call(bf16[8,128,128]{2,1,0:T(8,128)(2,1)} %bitcast.4, bf16[32,432]{1,0:T(8,128)(2,1)} %w1_hbm.1, bf16[64,864]{1,0:T(8,128)(2,1)} %w2_hbm.1, bf16[1728,128]{1,0:T(8,128)(2,1)} %bitcast.3), custom_call_target="tpu_custom_call" | custom-call | tf_op jit(solution)/shard_map/pallas_call | solution.py:311
  30.2 1.4 %copy.5 = bf16[8,2,1024]{2,1,0:T(2,128)(2,1)} copy(bf16[8,2,1024]{2,0,1:T(8,128)(2,1)} %bitcast.5) | data formatting | bytes 65536 | tf_op jit(solution)/shard_map/transpose | solution.py:337

commit v2 on v1

--- a/solution.py
+++ b/solution.py
@@ -15,6 +15,18 @@
 
 def iota(shape, axis):
     return lax.broadcasted_iota(jnp.int32, shape, axis)
+
+
+def start(copy):
+    copy.start()
+
+
+def receive(copy):
+    copy.wait_recv()
+
+
+def sent(copy):
+    copy.wait_send()
 
 
 def choose(rows, target):
@@ -98,10 +110,25 @@
     def at(dx, dy):
         return {"gx": lax.rem(g + dx + groups, groups), "yz": lax.rem(s + dy + shards, shards)}
 
+    def has(dx, dy):
+        x = {-1: g > 0, 0: None, 1: g < groups - 1}[dx]
+        y = {-1: s > 0, 0: None, 1: s < shards - 1}[dy]
+        return y if x is None else (x if y is None else x & y)
+
+    def each(copies, act, sign):
+        for (dx, dy), copy in zip(AROUND, copies):
+            pl.when(has(sign * dx, sign * dy))(functools.partial(act, copy))
+
     barrier = pltpu.get_barrier_semaphore()
-    partners = [(dx, dy) for dx, dy in AROUND if dx != 0] + [(0, k) for k in range(1, shards)]
-    for dx, dy in partners:
-        pl.semaphore_signal(barrier, inc=1, device_id=at(dx, dy), device_id_type=MESH)
+    count = shards - 1
+    for dx, dy in AROUND:
+        if dx != 0:
+            there = has(dx, dy)
+            count = count + there.astype(jnp.int32)
+            pl.when(there)(functools.partial(
+                pl.semaphore_signal, barrier, inc=1, device_id=at(dx, dy), device_id_type=MESH))
+    for k in range(1, shards):
+        pl.semaphore_signal(barrier, inc=1, device_id=at(0, k), device_id_type=MESH)
 
     loads = [
         pltpu.make_async_copy(v_hbm, p.at[1:9, 0:128], load_sem.at[0]),
@@ -121,7 +148,27 @@
             face[0, x + k] = cells[0:16, k * 128:(k + 1) * 128]
             face[1, x + k] = cells[16:32, k * 128:(k + 1) * 128]
 
-    pl.semaphore_wait(barrier, len(partners))
+    @pl.when(g == 0)
+    def _():
+        p[0] = jnp.zeros((160, 128), BF)
+        q[0:2] = jnp.zeros((2, 192, 128), BF)
+
+    @pl.when(g == groups - 1)
+    def _():
+        p[9] = jnp.zeros((160, 128), BF)
+        q[4:6] = jnp.zeros((2, 192, 128), BF)
+
+    @pl.when(s == 0)
+    def _():
+        p[:, 128:144, :] = jnp.zeros((10, 16, 128), BF)
+        q[:, 128:160, :] = jnp.zeros((6, 32, 128), BF)
+
+    @pl.when(s == shards - 1)
+    def _():
+        p[:, 144:160, :] = jnp.zeros((10, 16, 128), BF)
+        q[:, 160:192, :] = jnp.zeros((6, 32, 128), BF)
+
+    pl.semaphore_wait(barrier, count)
 
     first = []
     for k, (dx, dy) in enumerate(AROUND):
@@ -138,32 +185,14 @@
         first.append(pltpu.make_async_remote_copy(
             src_ref=src, dst_ref=dst, send_sem=s1.at[k], recv_sem=r1.at[k],
             device_id=at(dx, dy), device_id_type=MESH))
-    for copy in first:
-        copy.start()
+    each(first, start, 1)
 
     loads[1].wait()
     spread_one(w1, w1t)
     loads[2].wait()
     spread_two(w2, w2t)
 
-    for copy in first:
-        copy.wait_recv()
-
-    @pl.when(g == 0)
-    def _():
-        p[0] = jnp.zeros((160, 128), BF)
-
-    @pl.when(g == groups - 1)
-    def _():
-        p[9] = jnp.zeros((160, 128), BF)
-
-    @pl.when(s == 0)
-    def _():
-        p[:, 128:144, :] = jnp.zeros((10, 16, 128), BF)
-
-    @pl.when(s == shards - 1)
-    def _():
-        p[:, 144:160, :] = jnp.zeros((10, 16, 128), BF)
+    each(first, receive, -1)
 
     lane = iota((160, 128), 1)
     for x in range(10):
@@ -200,30 +229,12 @@
         second.append(pltpu.make_async_remote_copy(
             src_ref=q.at[2:4, rows], dst_ref=q.at[to, into], send_sem=s2.at[k], recv_sem=r2.at[k],
             device_id=at(dx, dy), device_id_type=MESH))
-    for copy in second:
-        copy.start()
+    each(second, start, 1)
 
     loads[3].wait()
     spread_three(shards, w3, w3t)
 
-    for copy in second:
-        copy.wait_recv()
-
-    @pl.when(g == 0)
-    def _():
-        q[0:2] = jnp.zeros((2, 192, 128), BF)
-
-    @pl.when(g == groups - 1)
-    def _():
-        q[4:6] = jnp.zeros((2, 192, 128), BF)
-
-    @pl.when(s == 0)
-    def _():
-        q[:, 128:160, :] = jnp.zeros((6, 32, 128), BF)
-
-    @pl.when(s == shards - 1)
-    def _():
-        q[:, 160:192, :] = jnp.zeros((6, 32, 128), BF)
+    each(second, receive, -1)
 
     lane = iota((192, 128), 1) & 63
     half = iota((192, 128), 1) < 64
@@ -276,29 +287,36 @@
     for k in range(1, shards):
         there = at(0, k)
         third.append(pltpu.make_async_remote_copy(
-            src_ref=out_s.at[there["yz"]], dst_ref=in_s.at[s], send_sem=s3.at[k], recv_sem=r3.at[k],
+            src_ref=out_s.at[there["yz"]], dst_ref=in_s.at[s], send_sem=s3.at[k], recv_sem=r3.at[s],
             device_id=there, device_id_type=MESH))
     for copy in third:
         copy.start()
     in_s[s] = out_s[s]
-    for copy in first + second:
-        copy.wait_send()
-    for copy in third:
-        copy.wait_recv()
+    each(first, sent, 1)
+    each(second, sent, 1)
 
     low = iota((size, 128), 1) < 64
     parity = (iota((size, 128), 1) & 32) == 0
-    done = []
-    for n in range(shards):
-        below = in_s[n - 1, size:, :].astype(F32) if n > 0 else jnp.zeros((size, 128), F32)
-        above = in_s[n + 1, size:, :].astype(F32) if n < shards - 1 else jnp.zeros((size, 128), F32)
-        whole = in_s[n, 0:size, :].astype(F32) + jnp.where(parity, below, above)
-        done.append(jnp.maximum(whole, 0.0))
-    for n in range(0, shards, 2):
-        at0 = jnp.where(low, done[n], pltpu.roll(done[n + 1], 64, 1))
-        at1 = jnp.where(low, pltpu.roll(done[n], 64, 1), done[n + 1])
-        o_ref[0, :, n * 64:n * 64 + 128] = at0.astype(BF)
-        o_ref[1, :, n * 64:n * 64 + 128] = at1.astype(BF)
+    nothing = jnp.zeros((size, 128), F32)
+    main, cross = [], [nothing]
+    for n in range(shards + 1):
+        if n < shards:
+            @pl.when(n != s)
+            def _():
+                pltpu.make_async_remote_copy(
+                    src_ref=out_s.at[0], dst_ref=in_s.at[n], send_sem=s3.at[0], recv_sem=r3.at[n],
+                    device_id=at(0, 1), device_id_type=MESH).wait_recv()
+            block = in_s[n].astype(F32)
+            main.append(block[0:size])
+            cross.append(block[size:])
+        else:
+            cross.append(nothing)
+        if n >= 2 and n % 2 == 0:
+            left, right = [
+                jnp.maximum(main[m] + jnp.where(parity, cross[m], cross[m + 2]), 0.0) for m in (n - 2, n - 1)]
+            lanes = slice(n * 64 - 128, n * 64)
+            o_ref[0, :, lanes] = jnp.where(low, left, pltpu.roll(right, 64, 1)).astype(BF)
+            o_ref[1, :, lanes] = jnp.where(low, pltpu.roll(left, 64, 1), right).astype(BF)
     for copy in third:
         copy.wait_send()
 

time: 31.8 us -> 31.3 us (0.984)
  the two profiles are of different devices: /device:TPU:1 before, /device:TPU:6 now
where the time goes in v2:
time: 31.3 us; the launch traced here: 31.1 us
  Pallas kernels  29.7 us (95%)
  local copies, waits for them, and re-layouts  1.41 us (5%)
    pallas_call x1, Pallas kernels, per_device(): pl.pallas_call(functools.partial(kernel, groups, shards), out_shape=jax.S...  29.7 us
    transpose x1, local copies, waits for them, and re-layouts, per_device(): return jnp.moveaxis(out, 0, 1)  1.41 us

profile of v2, /device:TPU:6, one launch (start us, length us, event | category | flops | bytes accessed | tf_op | source)
XLA Modules:
  0.0 31.1 jit_solution(10942080895384113252)
XLA Ops:
  0.0 29.7 %shard_map.46 = bf16[2,8,1024]{2,1,0:T(8,128)(2,1)} custom-call(bf16[8,128,128]{2,1,0:T(8,128)(2,1)} %bitcast.4, bf16[32,432]{1,0:T(8,128)(2,1)} %w1_hbm.1, bf16[64,864]{1,0:T(8,128)(2,1)} %w2_hbm.1, bf16[1728,128]{1,0:T(8,128)(2,1)} %bitcast.3), custom_call_target="tpu_custom_call" | custom-call | tf_op jit(solution)/shard_map/pallas_call | solution.py:329
  29.7 1.4 %copy.5 = bf16[8,2,1024]{2,1,0:T(2,128)(2,1)} copy(bf16[8,2,1024]{2,0,1:T(8,128)(2,1)} %bitcast.5) | data formatting | bytes 65536 | tf_op jit(solution)/shard_map/transpose | solution.py:355

commit v3 on v2

--- a/solution.py
+++ b/solution.py
@@ -102,7 +102,7 @@
 
 def kernel(groups, shards, v_hbm, w1_hbm, w2_hbm, w3_hbm, o_ref,
            p, w1, w2, w3, face, b1, w1t, q, b2e, b2o, w2t, w3t, out_s, in_s,
-           load_sem, s1, r1, s2, r2, s3, r3):
+           load_sem, s1, r1, s2, r2, s3, r3, known):
     g = lax.axis_index("gx")
     s = lax.axis_index("yz")
     size = 128 // shards
@@ -120,15 +120,27 @@
             pl.when(has(sign * dx, sign * dy))(functools.partial(act, copy))
 
     barrier = pltpu.get_barrier_semaphore()
-    count = shards - 1
+    count = 0
     for dx, dy in AROUND:
-        if dx != 0:
-            there = has(dx, dy)
-            count = count + there.astype(jnp.int32)
-            pl.when(there)(functools.partial(
-                pl.semaphore_signal, barrier, inc=1, device_id=at(dx, dy), device_id_type=MESH))
-    for k in range(1, shards):
-        pl.semaphore_signal(barrier, inc=1, device_id=at(0, k), device_id_type=MESH)
+        there = has(dx, dy)
+        count = count + there.astype(jnp.int32)
+        pl.when(there)(functools.partial(
+            pl.semaphore_signal, barrier, inc=1, device_id=at(dx, dy), device_id_type=MESH))
+
+    rounds = []
+    while 2 << len(rounds) < shards:
+        rounds.append(2 << len(rounds))
+
+    def tell(r):
+        for side, d in enumerate((-rounds[r], rounds[r])):
+            pl.when((s + d >= 0) & (s + d < shards))(functools.partial(
+                pl.semaphore_signal, known.at[r, side], inc=1,
+                device_id={"gx": g, "yz": lax.rem(s + d + shards, shards)}, device_id_type=MESH))
+
+    def hear(r):
+        for side, d in enumerate((rounds[r], -rounds[r])):
+            pl.when((s + d >= 0) & (s + d < shards))(functools.partial(
+                pl.semaphore_wait, known.at[r, side], 1))
 
     loads = [
         pltpu.make_async_copy(v_hbm, p.at[1:9, 0:128], load_sem.at[0]),
@@ -193,6 +205,7 @@
     spread_two(w2, w2t)
 
     each(first, receive, -1)
+    tell(0)
 
     lane = iota((160, 128), 1)
     for x in range(10):
@@ -234,6 +247,9 @@
     loads[3].wait()
     spread_three(shards, w3, w3t)
 
+    for r in range(len(rounds) - 1):
+        hear(r)
+        tell(r + 1)
     each(second, receive, -1)
 
     lane = iota((192, 128), 1) & 63
@@ -289,6 +305,7 @@
         third.append(pltpu.make_async_remote_copy(
             src_ref=out_s.at[there["yz"]], dst_ref=in_s.at[s], send_sem=s3.at[k], recv_sem=r3.at[s],
             device_id=there, device_id_type=MESH))
+    hear(len(rounds) - 1)
     for copy in third:
         copy.start()
     in_s[s] = out_s[s]
@@ -349,6 +366,7 @@
             dma((4,)),
             dma((8,)), dma((8,)), dma((8,)), dma((8,)),
             dma((shards,)), dma((shards,)),
+            pltpu.SemaphoreType.REGULAR((8, 2)),
         ],
         compiler_params=pltpu.CompilerParams(collective_id=0, has_side_effects=True),
     )(volume.reshape(8, 128, 128), weight_one, weight_two, weight_three.T)

time: 31.3 us -> 31.1 us (level)
  no operation moved by 1% of the time
where the time goes in v3:
time: 31.1 us; the launch traced here: 31 us
  Pallas kernels  29.5 us (95%)
  local copies, waits for them, and re-layouts  1.41 us (5%)
    pallas_call x1, Pallas kernels, per_device(): pl.pallas_call(functools.partial(kernel, groups, shards), out_shape=jax.S...  29.5 us
    transpose x1, local copies, waits for them, and re-layouts, per_device(): return jnp.moveaxis(out, 0, 1)  1.41 us

profile of v3, /device:TPU:6, one launch (start us, length us, event | category | flops | bytes accessed | tf_op | source)
XLA Modules:
  0.0 31.0 jit_solution(16339905591142548625)
XLA Ops:
  0.0 29.5 %shard_map.46 = bf16[2,8,1024]{2,1,0:T(8,128)(2,1)} custom-call(bf16[8,128,128]{2,1,0:T(8,128)(2,1)} %bitcast.4, bf16[32,432]{1,0:T(8,128)(2,1)} %w1_hbm.1, bf16[64,864]{1,0:T(8,128)(2,1)} %w2_hbm.1, bf16[1728,128]{1,0:T(8,128)(2,1)} %bitcast.3), custom_call_target="tpu_custom_call" | custom-call | tf_op jit(solution)/shard_map/pallas_call | solution.py:346
  29.5 1.4 %copy.5 = bf16[8,2,1024]{2,1,0:T(2,128)(2,1)} copy(bf16[8,2,1024]{2,0,1:T(8,128)(2,1)} %bitcast.5) | data formatting | bytes 65536 | tf_op jit(solution)/shard_map/transpose | solution.py:373

commit v4 on v3

--- a/solution.py
+++ b/solution.py
@@ -10,7 +10,8 @@
 MESH = pl.DeviceIdType.MESH
 BF = jnp.bfloat16
 F32 = jnp.float32
-AROUND = tuple((dx, dy) for dx in (-1, 0, 1) for dy in (-1, 0, 1) if (dx, dy) != (0, 0))
+BESIDE = ((-1, 0), (1, 0))
+AROUND = ((-1, -1), (-1, 1), (1, -1), (1, 1), (0, -1), (0, 1)) + BESIDE
 
 
 def iota(shape, axis):
@@ -46,11 +47,11 @@
 
 def spread_one(w1, w1t):
     column = iota((1, 480), 1)
-    c = (column >= 160).astype(jnp.int32) + (column >= 320).astype(jnp.int32)
-    pos = column - 160 * c
-    own = pos < 128
-    y = jnp.where(own, pos & 7, jnp.where(pos < 144, -1, 8))
-    i = jnp.where(own, pos >> 3, pos & 15)
+    own = column < 384
+    edge = column & 31
+    c = jnp.where(own, column >> 7, (column - 384) >> 5)
+    y = jnp.where(own, column & 7, jnp.where(edge < 16, -1, 8))
+    i = jnp.where(own, (column & 127) >> 3, column & 15)
     for out in range(8):
         b = y - out + 1
         target = jnp.where((b >= 0) & (b <= 2), 32 + b * 48 + c * 16 + i, -1)
@@ -63,11 +64,11 @@
 
 def spread_two(w2, w2t):
     column = iota((1, 576), 1)
-    c = (column >= 192).astype(jnp.int32) + (column >= 384).astype(jnp.int32)
-    pos = column - 192 * c
-    group = pos >> 5
-    y = jnp.where(group < 4, group, jnp.where(group == 4, -1, 4))
-    i = pos & 31
+    own = column < 384
+    edge = column & 63
+    c = jnp.where(own, column >> 7, (column - 384) >> 6)
+    y = jnp.where(own, (column & 127) >> 5, jnp.where(edge < 32, -1, 4))
+    i = column & 31
     for out in range(4):
         b = y - out + 1
         target = jnp.where((b >= 0) & (b <= 2), 64 + b * 96 + c * 32 + i, -1)
@@ -101,7 +102,7 @@
 
 
 def kernel(groups, shards, v_hbm, w1_hbm, w2_hbm, w3_hbm, o_ref,
-           p, w1, w2, w3, face, b1, w1t, q, b2e, b2o, w2t, w3t, out_s, in_s,
+           p, w1, w2, w3, face, b1, h1, a1, w1t, q, b2e, b2o, h2e, h2o, a2, w2t, w3t, out_s, in_s,
            load_sem, s1, r1, s2, r2, s3, r3, known):
     g = lax.axis_index("gx")
     s = lax.axis_index("yz")
@@ -115,9 +116,10 @@
         y = {-1: s > 0, 0: None, 1: s < shards - 1}[dy]
         return y if x is None else (x if y is None else x & y)
 
-    def each(copies, act, sign):
+    def each(copies, act, sign, among=AROUND):
         for (dx, dy), copy in zip(AROUND, copies):
-            pl.when(has(sign * dx, sign * dy))(functools.partial(act, copy))
+            if (dx, dy) in among:
+                pl.when(has(sign * dx, sign * dy))(functools.partial(act, copy))
 
     barrier = pltpu.get_barrier_semaphore()
     count = 0
@@ -204,45 +206,73 @@
     loads[2].wait()
     spread_two(w2, w2t)
 
-    each(first, receive, -1)
+    lane = iota((128, 128), 1)
+    narrow = iota((32, 128), 1)
+
+    def lay_one(x):
+        mid = p[x, 0:128, :]
+        up, down = shifted(mid, lane, 0, 127)
+        b1[x, 0:128] = up
+        b1[x, 128:256] = mid
+        b1[x, 256:384] = down
+
+    def two(ref, x):
+        return jnp.concatenate([ref[x], ref[x + 1]], axis=1)
+
+    for x in range(1, 9):
+        lay_one(x)
+    for k, taps in enumerate(((1, 2), (0, 1, 2), (0, 1, 2), (0, 1))):
+        total = None
+        for a in taps:
+            part = dot(w1t[a, :, 0:384], two(b1, 2 * k + a))
+            total = part if total is None else total + part
+        a1[k] = total
+    a1[0, :, 128:256] += dot(w1t[0, :, 0:384], b1[1])
+    a1[3, :, 0:128] += dot(w1t[2, :, 0:384], b1[8])
+
+    each(first, receive, -1, BESIDE)
+    lay_one(0)
+    lay_one(9)
+    a1[0, :, 0:128] += dot(w1t[0, :, 0:384], b1[0])
+    a1[3, :, 128:256] += dot(w1t[2, :, 0:384], b1[9])
+    each(first, receive, -1, AROUND[:6])
     tell(0)
-
-    lane = iota((160, 128), 1)
     for x in range(10):
-        mid = p[x]
-        up, down = shifted(mid, lane, 0, 127)
-        b1[x, 0:160] = up
-        b1[x, 160:320] = mid
-        b1[x, 320:480] = down
-    pooled = []
-    for x in range(0, 8, 2):
-        total = None
-        for a in range(3):
-            part = dot(w1t[a], jnp.concatenate([b1[x + a], b1[x + a + 1]], axis=1))
-            total = part if total is None else total + part
-        total = jnp.maximum(total, 0.0)
-        total = total[0:128] + total[128:256]
-        total = total[:, 0:128] + total[:, 128:256]
-        total = (total + pltpu.roll(total, 127, 1)) * 0.125
-        pooled.append(total.astype(BF))
+        mid = p[x, 128:160, :]
+        up, down = shifted(mid, narrow, 0, 127)
+        h1[x, 0:32] = up
+        h1[x, 32:64] = mid
+        h1[x, 64:96] = down
     lanes = iota((256, 128), 1)
     pick = jnp.where(iota((256, 128), 0) == (lanes >> 6) * 128 + (lanes & 63) * 2, 1.0, 0.0).astype(BF)
+
+    second = []
     for j in range(2):
-        q[2 + j, 0:128, :] = dot(jnp.concatenate(pooled[2 * j:2 * j + 2], axis=1), pick).astype(BF)
-
-    second = []
-    for k, (dx, dy) in enumerate(AROUND):
-        to = slice(2, 4) if dx == 0 else (slice(0, 2) if dx > 0 else slice(4, 6))
-        if dy == 0:
-            rows, into = slice(0, 128), slice(0, 128)
-        elif dy > 0:
-            rows, into = slice(96, 128), slice(128, 160)
-        else:
-            rows, into = slice(0, 32), slice(160, 192)
-        second.append(pltpu.make_async_remote_copy(
-            src_ref=q.at[2:4, rows], dst_ref=q.at[to, into], send_sem=s2.at[k], recv_sem=r2.at[k],
-            device_id=at(dx, dy), device_id_type=MESH))
-    each(second, start, 1)
+        pooled = []
+        for k in (2 * j, 2 * j + 1):
+            total = a1[k]
+            for a in range(3):
+                total += dot(w1t[a, :, 384:480], two(h1, 2 * k + a))
+            total = jnp.maximum(total, 0.0)
+            total = total[0:128] + total[128:256]
+            total = total[:, 0:128] + total[:, 128:256]
+            total = (total + pltpu.roll(total, 127, 1)) * 0.125
+            pooled.append(total.astype(BF))
+        q[2 + j, 0:128, :] = dot(jnp.concatenate(pooled, axis=1), pick).astype(BF)
+        half = []
+        for k, (dx, dy) in enumerate(AROUND):
+            to = 2 + j - 2 * dx
+            if dy == 0:
+                rows, into = slice(0, 128), slice(0, 128)
+            elif dy > 0:
+                rows, into = slice(96, 128), slice(128, 160)
+            else:
+                rows, into = slice(0, 32), slice(160, 192)
+            half.append(pltpu.make_async_remote_copy(
+                src_ref=q.at[2 + j, rows], dst_ref=q.at[to, into], send_sem=s2.at[8 * j + k],
+                recv_sem=r2.at[8 * j + k], device_id=at(dx, dy), device_id_type=MESH))
+        each(half, start, 1)
+        second.append(half)
 
     loads[3].wait()
     spread_three(shards, w3, w3t)
@@ -250,27 +280,39 @@
     for r in range(len(rounds) - 1):
         hear(r)
         tell(r + 1)
-    each(second, receive, -1)
-
-    lane = iota((192, 128), 1) & 63
-    half = iota((192, 128), 1) < 64
-    for j in range(5):
-        if j > 0:
-            mid = q[j]
+    lane = iota((128, 128), 1) & 63
+    low = iota((128, 128), 1) < 64
+
+    def lay_two(even, odd, rows, size, lane, low):
+        for j in range(5):
+            if j > 0:
+                mid = q[j, rows, :]
+                up, down = shifted(mid, lane, 0, 63)
+                even[j - 1, 0:size] = up
+                even[j - 1, size:2 * size] = mid
+                even[j - 1, 2 * size:3 * size] = down
+            mid = jnp.where(low, pltpu.roll(q[j, rows, :], 64, 1), pltpu.roll(q[j + 1, rows, :], 64, 1))
             up, down = shifted(mid, lane, 0, 63)
-            b2e[j - 1, 0:192] = up
-            b2e[j - 1, 192:384] = mid
-            b2e[j - 1, 384:576] = down
-        mid = jnp.where(half, pltpu.roll(q[j], 64, 1), pltpu.roll(q[j + 1], 64, 1))
-        up, down = shifted(mid, lane, 0, 63)
-        b2o[j, 0:192] = up
-        b2o[j, 192:384] = mid
-        b2o[j, 384:576] = down
+            odd[j, 0:size] = up
+            odd[j, size:2 * size] = mid
+            odd[j, 2 * size:3 * size] = down
+
+    def terms_two(even, odd, j, columns):
+        total = dot(w2t[0, :, columns], two(odd, j))
+        total += dot(w2t[1, :, columns], two(even, j))
+        return total + dot(w2t[2, :, columns], two(odd, j + 1))
+
+    for half in second:
+        each(half, receive, -1, BESIDE)
+    lay_two(b2e, b2o, slice(0, 128), 128, lane, low)
+    for j in range(2):
+        a2[j] = terms_two(b2e, b2o, 2 * j, slice(0, 384))
+    for half in second:
+        each(half, receive, -1, AROUND[:6])
+    lay_two(h2e, h2o, slice(128, 192), 64, lane[0:64], low[0:64])
     pooled = []
     for j in range(0, 4, 2):
-        total = dot(w2t[0], jnp.concatenate([b2o[j], b2o[j + 1]], axis=1))
-        total += dot(w2t[1], jnp.concatenate([b2e[j], b2e[j + 1]], axis=1))
-        total += dot(w2t[2], jnp.concatenate([b2o[j + 1], b2o[j + 2]], axis=1))
+        total = a2[j // 2] + terms_two(h2e, h2o, j, slice(384, 576))
         total = jnp.maximum(total, 0.0)
         total = total[0:128] + total[128:256]
         for k in range(2):
@@ -283,7 +325,6 @@
                 pair = jnp.where(g == groups - 1, 0.0, pair)
             pooled.append(pair)
 
-    low = iota((128, 128), 1) < 64
     stacked = jnp.concatenate(
         [jnp.where(low, pooled[a], pooled[a + 1]).astype(BF) for a in range(3)], axis=0)
     column = iota((1, 384), 1)
@@ -300,17 +341,24 @@
     out_s[...] = jnp.where(parity, even, odd).astype(BF).reshape(shards, 2 * size, 128)
 
     third = []
-    for k in range(1, shards):
-        there = at(0, k)
-        third.append(pltpu.make_async_remote_copy(
-            src_ref=out_s.at[there["yz"]], dst_ref=in_s.at[s], send_sem=s3.at[k], recv_sem=r3.at[s],
-            device_id=there, device_id_type=MESH))
+    deep = shards // 2
+    far = sorted(range(deep), key=lambda d: -min(d, deep - d))
+    for flip in (1, 0):
+        for d in far:
+            if (flip, d) == (0, 0):
+                continue
+            z = lax.rem(lax.div(s, 2) + d, deep)
+            there = 2 * z + (1 - lax.rem(s, 2) if flip else lax.rem(s, 2))
+            third.append(pltpu.make_async_remote_copy(
+                src_ref=out_s.at[there], dst_ref=in_s.at[s], send_sem=s3.at[len(third)], recv_sem=r3.at[s],
+                device_id={"gx": g, "yz": there}, device_id_type=MESH))
     hear(len(rounds) - 1)
     for copy in third:
         copy.start()
     in_s[s] = out_s[s]
     each(first, sent, 1)
-    each(second, sent, 1)
+    for half in second:
+        each(half, sent, 1)
 
     low = iota((size, 128), 1) < 64
     parity = (iota((size, 128), 1) & 32) == 0
@@ -354,17 +402,22 @@
             pltpu.VMEM((64, 864), BF),
             pltpu.VMEM((1728, 128), BF),
             pltpu.VMEM((2, 8, 16, 128), BF),
-            pltpu.VMEM((10, 480, 128), BF),
+            pltpu.VMEM((10, 384, 128), BF),
+            pltpu.VMEM((10, 96, 128), BF),
+            pltpu.VMEM((4, 256, 256), F32),
             pltpu.VMEM((3, 256, 480), BF),
             pltpu.VMEM((6, 192, 128), BF),
-            pltpu.VMEM((4, 576, 128), BF),
-            pltpu.VMEM((5, 576, 128), BF),
+            pltpu.VMEM((4, 384, 128), BF),
+            pltpu.VMEM((5, 384, 128), BF),
+            pltpu.VMEM((4, 192, 128), BF),
+            pltpu.VMEM((5, 192, 128), BF),
+            pltpu.VMEM((2, 256, 256), F32),
             pltpu.VMEM((3, 256, 576), BF),
             pltpu.VMEM((2, 256, 1152), BF),
             pltpu.VMEM((shards, 2 * size, 128), BF),
             pltpu.VMEM((shards, 2 * size, 128), BF),
             dma((4,)),
-            dma((8,)), dma((8,)), dma((8,)), dma((8,)),
+            dma((8,)), dma((8,)), dma((16,)), dma((16,)),
             dma((shards,)), dma((shards,)),
             pltpu.SemaphoreType.REGULAR((8, 2)),
         ],

time: 31.1 us -> 30.2 us (0.971)
  Pallas kernels: 29.5 us -> 28.7 us
    pallas_call x1, Pallas kernels: 29.5 us -> 28.7 us  [per_device(): pl.pallas_call(functools.partial(kernel, groups, shards), out_shape=jax.S...]
where the time goes in v4:
time: 30.2 us; the launch traced here: 30.1 us
  Pallas kernels  28.7 us (95%)
  local copies, waits for them, and re-layouts  1.41 us (5%)
    pallas_call x1, Pallas kernels, per_device(): pl.pallas_call(functools.partial(kernel, groups, shards), out_shape=jax.S...  28.7 us
    transpose x1, local copies, waits for them, and re-layouts, per_device(): return jnp.moveaxis(out, 0, 1)  1.41 us

profile of v4, /device:TPU:6, one launch (start us, length us, event | category | flops | bytes accessed | tf_op | source)
XLA Modules:
  0.0 30.1 jit_solution(8847752381652570951)
XLA Ops:
  0.0 28.7 %shard_map.46 = bf16[2,8,1024]{2,1,0:T(8,128)(2,1)} custom-call(bf16[8,128,128]{2,1,0:T(8,128)(2,1)} %bitcast.4, bf16[32,432]{1,0:T(8,128)(2,1)} %w1_hbm.1, bf16[64,864]{1,0:T(8,128)(2,1)} %w2_hbm.1, bf16[1728,128]{1,0:T(8,128)(2,1)} %bitcast.3), custom_call_target="tpu_custom_call" | custom-call | tf_op jit(solution)/shard_map/pallas_call | solution.py:394
  28.7 1.4 %copy.5 = bf16[8,2,1024]{2,1,0:T(2,128)(2,1)} copy(bf16[8,2,1024]{2,0,1:T(8,128)(2,1)} %bitcast.5) | data formatting | bytes 65536 | tf_op jit(solution)/shard_map/transpose | solution.py:426

commit v5 on v4

--- a/solution.py
+++ b/solution.py
@@ -230,34 +230,47 @@
     a1[0, :, 128:256] += dot(w1t[0, :, 0:384], b1[1])
     a1[3, :, 0:128] += dot(w1t[2, :, 0:384], b1[8])
 
+    lanes = iota((256, 128), 1)
+    pick = jnp.where(iota((256, 128), 0) == (lanes >> 6) * 128 + (lanes & 63) * 2, 1.0, 0.0).astype(BF)
+
     each(first, receive, -1, BESIDE)
     lay_one(0)
     lay_one(9)
     a1[0, :, 0:128] += dot(w1t[0, :, 0:384], b1[0])
     a1[3, :, 128:256] += dot(w1t[2, :, 0:384], b1[9])
-    each(first, receive, -1, AROUND[:6])
-    tell(0)
-    for x in range(10):
+
+    def edge_one(x):
         mid = p[x, 128:160, :]
         up, down = shifted(mid, narrow, 0, 127)
         h1[x, 0:32] = up
         h1[x, 32:64] = mid
         h1[x, 64:96] = down
-    lanes = iota((256, 128), 1)
-    pick = jnp.where(iota((256, 128), 0) == (lanes >> 6) * 128 + (lanes & 63) * 2, 1.0, 0.0).astype(BF)
+
+    def edge_terms(k, taps):
+        total = a1[k]
+        for a in taps:
+            total += dot(w1t[a, :, 384:480], two(h1, 2 * k + a))
+        return total
+
+    def pool_one(total):
+        total = jnp.maximum(total, 0.0)
+        total = total[0:128] + total[128:256]
+        total = total[:, 0:128] + total[:, 128:256]
+        return ((total + pltpu.roll(total, 127, 1)) * 0.125).astype(BF)
+
+    each(first, receive, -1, AROUND[4:6])
+    for x in range(1, 9):
+        edge_one(x)
+    inner = [pool_one(edge_terms(k, (0, 1, 2))) for k in (1, 2)]
+    a1[0] = edge_terms(0, (1, 2))
+    a1[3] = edge_terms(3, (0, 1))
+    each(first, receive, -1, AROUND[:4])
 
     second = []
     for j in range(2):
-        pooled = []
-        for k in (2 * j, 2 * j + 1):
-            total = a1[k]
-            for a in range(3):
-                total += dot(w1t[a, :, 384:480], two(h1, 2 * k + a))
-            total = jnp.maximum(total, 0.0)
-            total = total[0:128] + total[128:256]
-            total = total[:, 0:128] + total[:, 128:256]
-            total = (total + pltpu.roll(total, 127, 1)) * 0.125
-            pooled.append(total.astype(BF))
+        edge_one(9 * j)
+        outer = pool_one(edge_terms(3 * j, (2 * j,)))
+        pooled = [inner[1], outer] if j else [outer, inner[0]]
         q[2 + j, 0:128, :] = dot(jnp.concatenate(pooled, axis=1), pick).astype(BF)
         half = []
         for k, (dx, dy) in enumerate(AROUND):
@@ -274,6 +287,7 @@
         each(half, start, 1)
         second.append(half)
 
+    tell(0)
     loads[3].wait()
     spread_three(shards, w3, w3t)
 
@@ -301,6 +315,13 @@
         total = dot(w2t[0, :, columns], two(odd, j))
         total += dot(w2t[1, :, columns], two(even, j))
         return total + dot(w2t[2, :, columns], two(odd, j + 1))
+
+    column = iota((1, 384), 1)
+    c = column >> 7
+    inside = column & 127
+    z = (inside & 31) + c - 1
+    target = jnp.where((z >= 0) & (z < 32), (inside >> 6) * 64 + 2 * z, -1)
+    chosen = choose(128, target)
 
     for half in second:
         each(half, receive, -1, BESIDE)
@@ -327,12 +348,7 @@
 
     stacked = jnp.concatenate(
         [jnp.where(low, pooled[a], pooled[a + 1]).astype(BF) for a in range(3)], axis=0)
-    column = iota((1, 384), 1)
-    c = column >> 7
-    inside = column & 127
-    z = (inside & 31) + c - 1
-    target = jnp.where((z >= 0) & (z < 32), (inside >> 6) * 64 + 2 * z, -1)
-    planes = dot(stacked, choose(128, target)).astype(BF)
+    planes = dot(stacked, chosen).astype(BF)
     right = jnp.concatenate(
         [planes[a * 128:(a + 1) * 128, c * 128:(c + 1) * 128] for a in range(3) for c in range(3)], axis=0)
     even = dot(w3t[0], right)

time: 30.2 us -> 30.6 us (1.013)
  Pallas kernels: 28.7 us -> 29.1 us
    pallas_call x1, Pallas kernels: 28.7 us -> 29.1 us  [per_device(): pl.pallas_call(functools.partial(kernel, groups, shards), out_shape=jax.S...]
where the time goes in v5:
time: 30.6 us; the launch traced here: 30.5 us
  Pallas kernels  29.1 us (95%)
  local copies, waits for them, and re-layouts  1.41 us (5%)
    pallas_call x1, Pallas kernels, per_device(): pl.pallas_call(functools.partial(kernel, groups, shards), out_shape=jax.S...  29.1 us
    transpose x1, local copies, waits for them, and re-layouts, per_device(): return jnp.moveaxis(out, 0, 1)  1.41 us

profile of v5, /device:TPU:6, one launch (start us, length us, event | category | flops | bytes accessed | tf_op | source)
XLA Modules:
  0.0 30.5 jit_solution(10560301638327367551)
XLA Ops:
  0.0 29.1 %shard_map.46 = bf16[2,8,1024]{2,1,0:T(8,128)(2,1)} custom-call(bf16[8,128,128]{2,1,0:T(8,128)(2,1)} %bitcast.4, bf16[32,432]{1,0:T(8,128)(2,1)} %w1_hbm.1, bf16[64,864]{1,0:T(8,128)(2,1)} %w2_hbm.1, bf16[1728,128]{1,0:T(8,128)(2,1)} %bitcast.3), custom_call_target="tpu_custom_call" | custom-call | tf_op jit(solution)/shard_map/pallas_call | solution.py:410
  29.1 1.4 %copy.5 = bf16[8,2,1024]{2,1,0:T(2,128)(2,1)} copy(bf16[8,2,1024]{2,0,1:T(8,128)(2,1)} %bitcast.5) | data formatting | bytes 65536 | tf_op jit(solution)/shard_map/transpose | solution.py:442

commit v6 on v4

--- a/solution.py
+++ b/solution.py
@@ -11,6 +11,8 @@
 BF = jnp.bfloat16
 F32 = jnp.float32
 BESIDE = ((-1, 0), (1, 0))
+PIECES = ((1, -1, None), (1, 1, None), (0, -1, (0, 5)), (0, 1, (0, 5)), (-1, -1, None), (-1, 1, None),
+          (0, -1, (5, 8)), (0, 1, (5, 8)), (-1, 0, None), (1, 0, None))
 AROUND = ((-1, -1), (-1, 1), (1, -1), (1, 1), (0, -1), (0, 1)) + BESIDE
 
 
@@ -121,6 +123,10 @@
             if (dx, dy) in among:
                 pl.when(has(sign * dx, sign * dy))(functools.partial(act, copy))
 
+    def pieces(copies, act, sign, low, high):
+        for (dx, dy, _), copy in zip(PIECES[low:high], copies[low:high]):
+            pl.when(has(sign * dx, sign * dy))(functools.partial(act, copy))
+
     barrier = pltpu.get_barrier_semaphore()
     count = 0
     for dx, dy in AROUND:
@@ -185,7 +191,7 @@
     pl.semaphore_wait(barrier, count)
 
     first = []
-    for k, (dx, dy) in enumerate(AROUND):
+    for k, (dx, dy, part) in enumerate(PIECES):
         plane = 7 if dx > 0 else 0
         to = 0 if dx > 0 else 9
         side = 1 if dy > 0 else 0
@@ -193,13 +199,14 @@
         if dy == 0:
             src, dst = p.at[1 + plane, 0:128], p.at[to, 0:128]
         elif dx == 0:
-            src, dst = face.at[side], p.at[1:9, rows]
+            low, high = part
+            src, dst = face.at[side, low:high], p.at[1 + low:1 + high, rows]
         else:
             src, dst = face.at[side, plane], p.at[to, rows]
         first.append(pltpu.make_async_remote_copy(
             src_ref=src, dst_ref=dst, send_sem=s1.at[k], recv_sem=r1.at[k],
             device_id=at(dx, dy), device_id_type=MESH))
-    each(first, start, 1)
+    pieces(first, start, 1, 0, 10)
 
     loads[1].wait()
     spread_one(w1, w1t)
@@ -230,24 +237,23 @@
     a1[0, :, 128:256] += dot(w1t[0, :, 0:384], b1[1])
     a1[3, :, 0:128] += dot(w1t[2, :, 0:384], b1[8])
 
-    each(first, receive, -1, BESIDE)
+    lanes = iota((256, 128), 1)
+    pick = jnp.where(iota((256, 128), 0) == (lanes >> 6) * 128 + (lanes & 63) * 2, 1.0, 0.0).astype(BF)
+
+    pieces(first, receive, -1, 8, 10)
     lay_one(0)
     lay_one(9)
     a1[0, :, 0:128] += dot(w1t[0, :, 0:384], b1[0])
     a1[3, :, 128:256] += dot(w1t[2, :, 0:384], b1[9])
-    each(first, receive, -1, AROUND[:6])
-    tell(0)
-    for x in range(10):
-        mid = p[x, 128:160, :]
-        up, down = shifted(mid, narrow, 0, 127)
-        h1[x, 0:32] = up
-        h1[x, 32:64] = mid
-        h1[x, 64:96] = down
-    lanes = iota((256, 128), 1)
-    pick = jnp.where(iota((256, 128), 0) == (lanes >> 6) * 128 + (lanes & 63) * 2, 1.0, 0.0).astype(BF)
-
     second = []
     for j in range(2):
+        pieces(first, receive, -1, 4 * j, 4 * j + 4)
+        for x in range(6 * j, 6 + 4 * j):
+            mid = p[x, 128:160, :]
+            up, down = shifted(mid, narrow, 0, 127)
+            h1[x, 0:32] = up
+            h1[x, 32:64] = mid
+            h1[x, 64:96] = down
         pooled = []
         for k in (2 * j, 2 * j + 1):
             total = a1[k]
@@ -274,6 +280,7 @@
         each(half, start, 1)
         second.append(half)
 
+    tell(0)
     loads[3].wait()
     spread_three(shards, w3, w3t)
 
@@ -301,6 +308,13 @@
         total = dot(w2t[0, :, columns], two(odd, j))
         total += dot(w2t[1, :, columns], two(even, j))
         return total + dot(w2t[2, :, columns], two(odd, j + 1))
+
+    column = iota((1, 384), 1)
+    c = column >> 7
+    inside = column & 127
+    z = (inside & 31) + c - 1
+    target = jnp.where((z >= 0) & (z < 32), (inside >> 6) * 64 + 2 * z, -1)
+    chosen = choose(128, target)
 
     for half in second:
         each(half, receive, -1, BESIDE)
@@ -327,12 +341,7 @@
 
     stacked = jnp.concatenate(
         [jnp.where(low, pooled[a], pooled[a + 1]).astype(BF) for a in range(3)], axis=0)
-    column = iota((1, 384), 1)
-    c = column >> 7
-    inside = column & 127
-    z = (inside & 31) + c - 1
-    target = jnp.where((z >= 0) & (z < 32), (inside >> 6) * 64 + 2 * z, -1)
-    planes = dot(stacked, choose(128, target)).astype(BF)
+    planes = dot(stacked, chosen).astype(BF)
     right = jnp.concatenate(
         [planes[a * 128:(a + 1) * 128, c * 128:(c + 1) * 128] for a in range(3) for c in range(3)], axis=0)
     even = dot(w3t[0], right)
@@ -356,7 +365,7 @@
     for copy in third:
         copy.start()
     in_s[s] = out_s[s]
-    each(first, sent, 1)
+    pieces(first, sent, 1, 0, 10)
     for half in second:
         each(half, sent, 1)
 
@@ -417,11 +426,12 @@
             pltpu.VMEM((shards, 2 * size, 128), BF),
             pltpu.VMEM((shards, 2 * size, 128), BF),
             dma((4,)),
-            dma((8,)), dma((8,)), dma((16,)), dma((16,)),
+            dma((10,)), dma((10,)), dma((16,)), dma((16,)),
             dma((shards,)), dma((shards,)),
             pltpu.SemaphoreType.REGULAR((8, 2)),
         ],
-        compiler_params=pltpu.CompilerParams(collective_id=0, has_side_effects=True),
+        compiler_params=pltpu.CompilerParams(
+            collective_id=0, has_side_effects=True, vmem_limit_bytes=56510000),
     )(volume.reshape(8, 128, 128), weight_one, weight_two, weight_three.T)
     return jnp.moveaxis(out, 0, 1)
 

time: 30.2 us -> 28.7 us (0.950)
  local copies, waits for them, and re-layouts: 1.41 us -> 0.65 us
  Pallas kernels: 28.7 us -> 28 us
    transpose x1, local copies, waits for them, and re-layouts: 1.41 us -> 0.65 us  [per_device(): return jnp.moveaxis(out, 0, 1)]
    pallas_call x1, Pallas kernels: 28.7 us -> 28 us  [per_device(): pl.pallas_call(functools.partial(kernel, groups, shards), out_shape=jax.S...]
where the time goes in v6:
time: 28.7 us; the launch traced here: 28.6 us
  Pallas kernels  28 us (98%)
  local copies, waits for them, and re-layouts  0.65 us (2%)
    pallas_call x1, Pallas kernels, per_device(): pl.pallas_call(functools.partial(kernel, groups, shards), out_shape=jax.S...  28 us
    transpose x1, local copies, waits for them, and re-layouts, per_device(): return jnp.moveaxis(out, 0, 1)  0.65 us

profile of v6, /device:TPU:6, one launch (start us, length us, event | category | flops | bytes accessed | tf_op | source)
XLA Modules:
  0.0 28.6 jit_solution(13374004197937625313)
XLA Ops:
  0.0 28.0 %shard_map.46 = bf16[2,8,1024]{2,1,0:T(8,128)(2,1)S(1)} custom-call(bf16[8,128,128]{2,1,0:T(8,128)(2,1)} %bitcast.5, bf16[32,432]{1,0:T(8,128)(2,1)} %w1_hbm.1, bf16[64,864]{1,0:T(8,128)(2,1)} %w2_hbm.1, bf16[1728,128]{1,0:T(8,128)(2,1)} %bitcast.4), custom_call_target="tpu_custom_call" | custom-call | tf_op jit(solution)/shard_map/pallas_call | solution.py:403
  28.0 0.6 %copy.5 = bf16[8,2,1024]{2,1,0:T(2,128)(2,1)} copy(bf16[8,2,1024]{2,0,1:T(8,128)(2,1)S(1)} %bitcast.3) | data formatting | bytes 65536 | tf_op jit(solution)/shard_map/transpose | solution.py:436

commit v7 on v6

--- a/solution.py
+++ b/solution.py
@@ -156,10 +156,11 @@
         pltpu.make_async_copy(w2_hbm, w2, load_sem.at[2]),
         pltpu.make_async_copy(w3_hbm, w3, load_sem.at[3]),
     ]
-    for load in loads:
+    loads[0].start()
+
+    loads[0].wait()
+    for load in loads[1:]:
         load.start()
-
-    loads[0].wait()
     which = iota((32, 128), 0)
     ends = jnp.where(iota((32, 128), 1) == (which & 15) * 8 + (which >> 4) * 7, 1.0, 0.0).astype(BF)
     for x in range(0, 8, 2):

time: 28.7 us -> 28.8 us (level)
  no operation moved by 1% of the time
where the time goes in v7:
time: 28.8 us; the launch traced here: 28.6 us
  Pallas kernels  28 us (97%)
  local copies, waits for them, and re-layouts  0.65 us (2%)
    pallas_call x1, Pallas kernels, per_device(): pl.pallas_call(functools.partial(kernel, groups, shards), out_shape=jax.S...  28 us
    transpose x1, local copies, waits for them, and re-layouts, per_device(): return jnp.moveaxis(out, 0, 1)  0.65 us

profile of v7, /device:TPU:6, one launch (start us, length us, event | category | flops | bytes accessed | tf_op | source)
XLA Modules:
  0.0 28.6 jit_solution(18359884755187428836)
XLA Ops:
  0.0 28.0 %shard_map.46 = bf16[2,8,1024]{2,1,0:T(8,128)(2,1)S(1)} custom-call(bf16[8,128,128]{2,1,0:T(8,128)(2,1)} %bitcast.5, bf16[32,432]{1,0:T(8,128)(2,1)} %w1_hbm.1, bf16[64,864]{1,0:T(8,128)(2,1)} %w2_hbm.1, bf16[1728,128]{1,0:T(8,128)(2,1)} %bitcast.4), custom_call_target="tpu_custom_call" | custom-call | tf_op jit(solution)/shard_map/pallas_call | solution.py:404
  28.0 0.6 %copy.5 = bf16[8,2,1024]{2,1,0:T(2,128)(2,1)} copy(bf16[8,2,1024]{2,0,1:T(8,128)(2,1)S(1)} %bitcast.3) | data formatting | bytes 65536 | tf_op jit(solution)/shard_map/transpose | solution.py:437
